TPU v7x, 128 devices: a whole 4x4x4 slice. The times are simulated.
128 devices in a mesh: pix: 64 (over x, z, y_hi, core), col: 2 (over y_lo).
Axes of the slice: x: 4, y: 4 (y_hi: 2, y_lo: 2; y = y_hi * 2 + y_lo), z: 4, core: 2. Of those that a mesh axis runs over, the one named last changes fastest.
Arguments:
- observed: float32 [16384, 4096], P('pix', 'col'), may hold values from -40 to 40
- valid_mask: int32 [16384, 512], P('pix', 'col'), may hold values 0 or 1
- pix_factor: float32 [16384, 256], P('pix'), may hold values from -6 to 6
- col_factor: float32 [4096, 256], P('col'), may hold values from -0.375 to 0.375
Outputs:
- pix_next: float32 [16384, 256], P('pix')
- col_next: float32 [4096, 256], P('col')
- cloud: float32 [16384, 4096], P('pix', 'col')
All inputs are finite; a program needn't handle non-finite values. No bound on the sum of `valid_mask` on one device may be relied on, other than what follows from the above.
Results may differ from a plain program's by a relative error of at most 0.0003.
Values sent between devices are 32-bit elements; how exact they have to be, the bound alone decides.
A program may use at most 64 MiB of HBM per device.

v0:
```python
import jax
import jax.numpy as jnp
from jax import lax
from jax.sharding import PartitionSpec as P

BANDS = 8
WIDTH = 256
ITERS = 2
PASSES = 2
highest = lax.Precision.HIGHEST
threshold_scale = 1.0
diffusion = 0.2


def passed_along(block, axis, distance):
    devices = range(lax.axis_size(axis))
    route = [(i - distance, i) for i in devices if i - distance in devices]
    return lax.ppermute(block, axis, route)


def soft_cut(values, level):
    return jnp.sign(values) * jnp.maximum(jnp.abs(values) - level, 0.0)


def flux_of(diff, level):
    return diff / (1.0 + (diff / level) ** 2)


def level_of(residual, weight, total):
    spread = lax.psum(jnp.sum(weight * residual * residual), ("pix", "col"))
    return threshold_scale * jnp.sqrt(spread / total + 1e-06)


def smooth_pass(grid, level, strip_index, pix_count):
    has_north = strip_index > 0
    has_south = strip_index < pix_count - 1
    top_row = grid[0]
    bottom_row = grid[-1]
    north_rim = passed_along(bottom_row, "pix", 1)
    south_rim = passed_along(top_row, "pix", -1)
    north_rim = jnp.where(has_north, north_rim, top_row)
    south_rim = jnp.where(has_south, south_rim, bottom_row)
    north = jnp.concatenate([north_rim[None], grid[:-1]], axis=0)
    south = jnp.concatenate([grid[1:], south_rim[None]], axis=0)
    west = jnp.concatenate([grid[:, :1], grid[:, :-1]], axis=1)
    east = jnp.concatenate([grid[:, 1:], grid[:, -1:]], axis=1)
    summed = flux_of(north - grid, level) + flux_of(south - grid, level)
    summed = summed + flux_of(west - grid, level) + flux_of(east - grid, level)
    return grid + diffusion * summed


def per_device(observed, valid_mask, pix_factor, col_factor):
    pix_count = lax.axis_size("pix")
    col_count = lax.axis_size("col")
    pixels, columns = observed.shape
    dates = valid_mask.shape[1]
    weight = jnp.broadcast_to(
        valid_mask.astype(jnp.float32)[:, :, None], (pixels, dates, BANDS)
    ).reshape(pixels, columns)
    total = float(pixels * columns * pix_count * col_count)
    pix_fac = pix_factor
    col_fac = col_factor
    low_rank = jnp.dot(pix_fac, col_fac.T, precision=highest)
    for iteration in range(ITERS):
        residual = observed - low_rank
        level = level_of(residual, weight, total)
        sparse = weight * soft_cut(residual, level)
        misfit = weight * (sparse - residual)
        pix_grad = lax.psum(jnp.dot(misfit, col_fac, precision=highest), "col")
        change = jnp.dot(pix_grad, col_fac.T, precision=highest)
        norm_local = jnp.sum(pix_grad * pix_grad)
        curve_local = jnp.sum(weight * change * change)
        top_sum = lax.psum(norm_local, "pix")
        bottom_sum = lax.psum(curve_local, ("pix", "col"))
        step_pix = top_sum / bottom_sum
        pix_fac = pix_fac - step_pix * pix_grad
        low_rank = low_rank - step_pix * change
        misfit = weight * (sparse - (observed - low_rank))
        local_grad = lax.dot_general(
            misfit,
            pix_fac,
            (((0,), (0,)), ((), ())),
            precision=highest,
            preferred_element_type=jnp.float32,
        )
        col_grad = lax.psum(local_grad, "pix")
        shifted = jnp.dot(pix_fac, col_grad.T, precision=highest)
        norm_local = jnp.sum(col_grad * col_grad)
        curve_local = jnp.sum(weight * shifted * shifted)
        top_sum = lax.psum(norm_local, "col")
        bottom_sum = lax.psum(curve_local, ("pix", "col"))
        step_col = top_sum / bottom_sum
        col_fac = col_fac - step_col * col_grad
        low_rank = low_rank - step_col * shifted
    residual = observed - low_rank
    level = level_of(residual, weight, total)
    layer = weight * soft_cut(residual, level)
    strip_index = lax.axis_index("pix")
    grid = layer.reshape(pixels // WIDTH, WIDTH, columns)
    for sweep_index in range(PASSES):
        grid = smooth_pass(grid, level, strip_index, pix_count)
    return (pix_fac, col_fac, grid.reshape(pixels, columns))


def solution(mesh):
    in_specs = (P("pix", "col"), P("pix", "col"), P("pix", None), P("col", None))
    out_specs = (P("pix", None), P("col", None), P("pix", "col"))
    return jax.shard_map(
        per_device, mesh=mesh, in_specs=in_specs, out_specs=out_specs, check_vma=False
    )
```

profile of v0, /device:TPU:32, one launch (start us, length us, event | category | flops | bytes accessed | tf_op | source)
XLA Modules:
  0.0 2382.3 jit_solution(10405248718728174888)
XLA Ops:
  7.2 0.0 all-reduce.5.cloned.1.call-start
  7.2 1.0 convert_element_type.3
  8.2 0.1 copy.7
  8.3 1.5 broadcast_bitcast_fusion
  9.8 2.0 copy.10
  11.8 7.0 fusion
  18.7 65.8 %psum.105 = f32[]{:T(128)} all-reduce(f32[]{:T(128)} %get-tuple-element.8), channel_id=1, replica_groups=mesh['pix'=64,'col'=2] {'pix','col'}, use_global_device_ids=true, to_apply=%region_1.0 | all-reduce | flops 1 | bytes 8 | tf_op jit(solution)/shard_map/psum | solution.py:30
  85.2 5.7 fusion.20
  91.0 0.0 all-reduce.5.cloned.1.call-update
  91.0 0.0 all-reduce.7.cloned.1.call-start
  91.0 28.1 %all-reduce.5.cloned.1.call-done = f32[256,256]{1,0:T(8,128)} async-done(((f32[256,256]{1,0:T(8,128)}), f32[256,256]{1,0:T(8,128)}) %all-reduce.5.cloned.1.call-update) | async-done | bytes 262160 | tf_op jit(solution)/shard_map/psum | solution.py:69
  119.1 1.6 multiply_reduce_fusion.3
  120.7 156.7 %psum.107 = f32[]{:T(128)} all-reduce(f32[]{:T(128)} %multiply_reduce_fusion.3), channel_id=1, replica_groups=mesh['pix'=64,'col'=2] {'pix'}, use_global_device_ids=true, to_apply=%region_4.0 | all-reduce | flops 1 | bytes 8 | tf_op jit(solution)/shard_map/psum | solution.py:73
  277.5 5.6 fusion.1
  283.1 72.4 %psum.108 = f32[]{:T(128)} all-reduce(f32[]{:T(128)} %get-tuple-element.19), channel_id=1, replica_groups=mesh['pix'=64,'col'=2] {'pix','col'}, use_global_device_ids=true, to_apply=%region_6.0 | all-reduce | flops 1 | bytes 8 | tf_op jit(solution)/shard_map/psum | solution.py:74
  356.8 0.0 copy-done.6
  356.8 9.0 fusion.16
  365.8 0.0 all-reduce.7.cloned.1.call-update
  365.8 0.0 all-reduce.9.cloned.1.call-start
  365.9 638.4 %all-reduce.7.cloned.1.call-done = f32[2048,256]{1,0:T(8,128)} async-done(((f32[2048,256]{1,0:T(8,128)}), f32[2048,256]{1,0:T(8,128)}) %all-reduce.7.cloned.1.call-update) | async-done | bytes 2097168 | tf_op jit(solution)/shard_map/psum | solution.py:86
  1004.2 2.7 multiply_reduce_fusion.1
  1007.0 5.5 psum.110
  1012.5 5.5 fusion.2
  1018.0 68.9 %psum.111 = f32[]{:T(128)} all-reduce(f32[]{:T(128)} %get-tuple-element.21), channel_id=1, replica_groups=mesh['pix'=64,'col'=2] {'pix','col'}, use_global_device_ids=true, to_apply=%region_11.0 | all-reduce | flops 1 | bytes 8 | tf_op jit(solution)/shard_map/psum | solution.py:91
  1088.2 7.4 fusion.3
  1095.6 64.8 %psum.112 = f32[]{:T(128)} all-reduce(f32[]{:T(128)} %get-tuple-element.5), channel_id=1, replica_groups=mesh['pix'=64,'col'=2] {'pix','col'}, use_global_device_ids=true, to_apply=%region_13.0 | all-reduce | flops 1 | bytes 8 | tf_op jit(solution)/shard_map/psum | solution.py:30
  1161.1 0.0 copy-start.3
  1161.1 2.6 multiply_subtract_fusion.2
  1163.8 1.3 copy-done
  1165.1 3.5 fusion.11
  1168.7 0.0 all-reduce.9.cloned.1.call-update
  1168.7 0.0 all-reduce.11.cloned.1.call-start
  1168.7 27.3 %all-reduce.9.cloned.1.call-done = f32[256,256]{1,0:T(8,128)} async-done(((f32[256,256]{1,0:T(8,128)}), f32[256,256]{1,0:T(8,128)}) %all-reduce.9.cloned.1.call-update) | async-done | bytes 262160 | tf_op jit(solution)/shard_map/psum | solution.py:69
  1196.0 1.6 multiply_reduce_fusion.2
  1197.6 156.7 %psum.114 = f32[]{:T(128)} all-reduce(f32[]{:T(128)} %multiply_reduce_fusion.2), channel_id=1, replica_groups=mesh['pix'=64,'col'=2] {'pix'}, use_global_device_ids=true, to_apply=%region_16.0 | all-reduce | flops 1 | bytes 8 | tf_op jit(solution)/shard_map/psum | solution.py:73
  1354.3 5.6 fusion.4
  1359.9 72.4 %psum.115 = f32[]{:T(128)} all-reduce(f32[]{:T(128)} %get-tuple-element.23), channel_id=1, replica_groups=mesh['pix'=64,'col'=2] {'pix','col'}, use_global_device_ids=true, to_apply=%region_18.0 | all-reduce | flops 1 | bytes 8 | tf_op jit(solution)/shard_map/psum | solution.py:74
  1433.8 0.0 copy-start.4
  1433.8 9.1 fusion.7
  1442.9 0.0 all-reduce.11.cloned.1.call-update
  1442.9 638.5 %all-reduce.11.cloned.1.call-done = f32[2048,256]{1,0:T(8,128)} async-done(((f32[2048,256]{1,0:T(8,128)}), f32[2048,256]{1,0:T(8,128)}) %all-reduce.11.cloned.1.call-update) | async-done | bytes 2097168 | tf_op jit(solution)/shard_map/psum | solution.py:86
  2081.4 2.7 multiply_reduce_fusion
  2084.1 5.5 psum.117
  2089.7 5.5 fusion.5
  2095.2 69.0 %psum.118 = f32[]{:T(128)} all-reduce(f32[]{:T(128)} %get-tuple-element.25), channel_id=1, replica_groups=mesh['pix'=64,'col'=2] {'pix','col'}, use_global_device_ids=true, to_apply=%region_23.0 | all-reduce | flops 1 | bytes 8 | tf_op jit(solution)/shard_map/psum | solution.py:91
  2165.4 6.5 fusion.6
  2171.9 64.7 %psum.119 = f32[]{:T(128)} all-reduce(f32[]{:T(128)} %get-tuple-element.3), channel_id=1, replica_groups=mesh['pix'=64,'col'=2] {'pix','col'}, use_global_device_ids=true, to_apply=%region_25.0 | all-reduce | flops 1 | bytes 8 | tf_op jit(solution)/shard_map/psum | solution.py:30
  2237.3 3.7 multiply_multiply_fusion.7
  2241.0 3.5 collective-permute-start.1
  2244.6 1.9 collective-permute-start
  2246.5 0.9 slice_bitcast_fusion.7
  2247.4 2.5 slice_bitcast_fusion.3
  2249.9 38.5 %collective-permute-done.1 = f32[256,2048]{1,0:T(8,128)S(1)} collective-permute-done((f32[256,2048]{1,0:T(8,128)}, f32[256,2048]{1,0:T(8,128)S(1)}, u32[]{:S(2)}, u32[]{:S(2)}) %collective-permute-start.1) | collective-permute-done | bytes 2097184 | tf_op jit(solution)/shard_map/ppermute | solution.py:18
  2288.5 4.2 collective-permute-done
  2292.7 4.4 multiply_add_fusion.1
  2297.1 3.2 collective-permute-start.3
  2300.3 1.9 collective-permute-start.2
  2302.2 0.0 copy-done.1
  2302.2 0.0 copy-done.2
  2302.3 1.6 multiply_subtract_fusion
  2303.9 0.4 slice_bitcast_fusion.1
  2304.3 39.8 %collective-permute-done.3 = f32[256,2048]{1,0:T(8,128)S(1)} collective-permute-done((f32[256,2048]{1,0:T(8,128)S(1)}, f32[256,2048]{1,0:T(8,128)S(1)}, u32[]{:S(2)}, u32[]{:S(2)}) %collective-permute-start.3) | collective-permute-done | bytes 2097184 | tf_op jit(solution)/shard_map/ppermute | solution.py:18
  2344.1 27.9 %collective-permute-done.2 = f32[256,2048]{1,0:T(8,128)S(1)} collective-permute-done((f32[256,2048]{1,0:T(8,128)S(1)}, f32[256,2048]{1,0:T(8,128)S(1)}, u32[]{:S(2)}, u32[]{:S(2)}) %collective-permute-start.2) | collective-permute-done | bytes 2097184 | tf_op jit(solution)/shard_map/ppermute | solution.py:18
  2371.9 3.3 multiply_add_fusion
  (15 shorter events, 0.1 us)
Async XLA Ops:
  7.2 111.9 %all-reduce.5.cloned.1.call-start = ((), (), s32[]{:S(2)}) async-start(), calls=%async_computation | async-start | bytes 524288 | tf_op jit(solution)/shard_map/psum | solution.py:69
  9.8 2.0 copy-start.8
  91.0 913.3 %all-reduce.7.cloned.1.call-start = ((), (), s32[]{:S(2)}) async-start(), calls=%async_computation.1 | async-start | bytes 4194304 | tf_op jit(solution)/shard_map/psum | solution.py:86
  277.5 79.3 %copy-start.6 = (f32[256,256]{1,0:T(8,128)S(1)}, f32[256,256]{1,0:T(8,128)}, u32[]{:S(2)}) copy-start(f32[256,256]{1,0:T(8,128)} %all-reduce.5.cloned.1.call-done) | copy-start | bytes 786436
  365.8 830.2 %all-reduce.9.cloned.1.call-start = ((), (), s32[]{:S(2)}) async-start(), calls=%async_computation.2 | async-start | bytes 524288 | tf_op jit(solution)/shard_map/psum | solution.py:69
  1161.1 4.0 copy-start.3
  1163.8 1.4 copy-start
  1168.7 912.7 %all-reduce.11.cloned.1.call-start = ((), (), s32[]{:S(2)}) async-start(), calls=%async_computation.3 | async-start | bytes 4194304 | tf_op jit(solution)/shard_map/psum | solution.py:86
  1354.3 79.4 %copy-start.5 = (f32[256,256]{1,0:T(8,128)S(1)}, f32[256,256]{1,0:T(8,128)}, u32[]{:S(2)}) copy-start(f32[256,256]{1,0:T(8,128)} %all-reduce.9.cloned.1.call-done) | copy-start | bytes 786436
  1433.8 655.9 %copy-start.4 = (f32[256,256]{1,0:T(8,128)}, f32[256,256]{1,0:T(8,128)S(1)}, u32[]{:S(2)}) copy-start(f32[256,256]{1,0:T(8,128)S(1)} %multiply_subtract_fusion.7) | copy-start | bytes 786436
  2241.0 47.5 %collective-permute-start.1 = (f32[256,2048]{1,0:T(8,128)}, f32[256,2048]{1,0:T(8,128)S(1)}, u32[]{:S(2)}, u32[]{:S(2)}) collective-permute-start(f32[256,2048]{1,0:T(8,128)} %multiply_multiply_fusion.7), channel_id=1, source_target_pairs={{2,0},{4,2},{6,4},{8,6},{10,8},{12,10},{14,12},{16,14},{18,16},{20... | collective-permute-start | bytes 6291464 | tf_op jit(solution)/shard_map/ppermute | solution.py:18
  2244.6 48.2 %collective-permute-start = (f32[256,2048]{1,0:T(8,128)}, f32[256,2048]{1,0:T(8,128)}, u32[]{:S(2)}, u32[]{:S(2)}) collective-permute-start(f32[256,2048]{1,0:T(8,128)} %multiply_multiply_fusion.7), channel_id=1, source_target_pairs={{0,2},{2,4},{4,6},{6,8},{8,10},{10,12},{12,14},{14,16},{16,18},{18... | collective-permute-start | bytes 6291464 | tf_op jit(solution)/shard_map/ppermute | solution.py:18
  2288.5 4.3 copy-start.7
  2292.7 9.5 copy-start.1
  2292.7 9.5 copy-start.2
  2297.1 47.0 %collective-permute-start.3 = (f32[256,2048]{1,0:T(8,128)S(1)}, f32[256,2048]{1,0:T(8,128)S(1)}, u32[]{:S(2)}, u32[]{:S(2)}) collective-permute-start(f32[256,2048]{1,0:T(8,128)S(1)} %multiply_add_fusion.1), channel_id=1, source_target_pairs={{2,0},{4,2},{6,4},{8,6},{10,8},{12,10},{14,12},{16,14},{18,16},{20... | collective-permute-start | bytes 6291464 | tf_op jit(solution)/shard_map/ppermute | solution.py:18
  2300.3 71.6 %collective-permute-start.2 = (f32[256,2048]{1,0:T(8,128)S(1)}, f32[256,2048]{1,0:T(8,128)S(1)}, u32[]{:S(2)}, u32[]{:S(2)}) collective-permute-start(f32[256,2048]{1,0:T(8,128)S(1)} %multiply_add_fusion.1), channel_id=1, source_target_pairs={{0,2},{2,4},{4,6},{6,8},{8,10},{10,12},{12,14},{14,16},{16,18},{18... | collective-permute-start | bytes 6291464 | tf_op jit(solution)/shard_map/ppermute | solution.py:18
Sparse Core Ops, SparseCore 0:
  91.1 27.9 all-reduce.4
  366.0 638.2 all-reduce.6
  1168.8 27.1 all-reduce.8
  1443.0 638.2 all-reduce.10
where the time goes:
time: 2390 us; the launch traced here: 2380 us
  waiting for transfers between devices  1440 us (60%)
  blocking collectives  803 us (34%)
  matrix products  56.5 us (2%)
  other arithmetic  39.3 us (2%)
    psum x2, waiting for transfers between devices, per_device(): col_grad = lax.psum(local_grad, 'pix')  1280 us
    psum x2, blocking collectives, per_device(): top_sum = lax.psum(norm_local, 'pix')  313 us
    psum x4, blocking collectives, per_device(): bottom_sum = lax.psum(curve_local, ('pix', 'col'))  283 us
    psum x3, blocking collectives, level_of(): spread = lax.psum(jnp.sum(weight * residual * residual), ('pix', 'col'))  195 us
    ppermute x4, waiting for transfers between devices, passed_along(): return lax.ppermute(block, axis, route)  110 us
    psum x2, waiting for transfers between devices, per_device(): pix_grad = lax.psum(jnp.dot(misfit, col_fac, precision=highest), 'col')  55.3 us
  transfers between devices with their start and end apart: 8, of which 8 were waited for; matrix products, arithmetic and copies ran while one was open for 0% of the time, Pallas kernels for 0%

commit v1 on v0

--- a/solution.py
+++ b/solution.py
@@ -1,3 +1,4 @@
+import functools
 import jax
 import jax.numpy as jnp
 from jax import lax
@@ -10,6 +11,15 @@
 highest = lax.Precision.HIGHEST
 threshold_scale = 1.0
 diffusion = 0.2
+
+
+def advance_joints(in_array, chip_axis, link_axis):
+    for nth in (chip_axis, link_axis):
+        in_array = lax.psum(in_array, axis_name=nth)
+    return in_array
+
+
+slots_take = functools.partial(advance_joints, chip_axis="col", link_axis="pix")
 
 
 def passed_along(block, axis, distance):
@@ -71,7 +81,7 @@
         norm_local = jnp.sum(pix_grad * pix_grad)
         curve_local = jnp.sum(weight * change * change)
         top_sum = lax.psum(norm_local, "pix")
-        bottom_sum = lax.psum(curve_local, ("pix", "col"))
+        bottom_sum = slots_take(curve_local)
         step_pix = top_sum / bottom_sum
         pix_fac = pix_fac - step_pix * pix_grad
         low_rank = low_rank - step_pix * change

time: 2390 us -> 2270 us (0.950)
  blocking collectives: 803 us -> 667 us
    psum x4 -> x2, blocking collectives: 283 us -> 138 us  [per_device(): bottom_sum = lax.psum(curve_local, ('pix', 'col'))]
where the time goes in v1:
time: 2270 us; the launch traced here: 2260 us
  waiting for transfers between devices  1460 us (64%)
  blocking collectives  667 us (29%)
  matrix products  56.5 us (2%)
  other arithmetic  39.3 us (2%)
    psum x2, waiting for transfers between devices, per_device(): col_grad = lax.psum(local_grad, 'pix')  1290 us
    psum x2, blocking collectives, per_device(): top_sum = lax.psum(norm_local, 'pix')  312 us
    psum x3, blocking collectives, level_of(): spread = lax.psum(jnp.sum(weight * residual * residual), ('pix', 'col'))  195 us
    psum x2, blocking collectives, per_device(): bottom_sum = lax.psum(curve_local, ('pix', 'col'))  138 us
    ppermute x4, waiting for transfers between devices, passed_along(): return lax.ppermute(block, axis, route)  110 us
    psum x2, waiting for transfers between devices, per_device(): pix_grad = lax.psum(jnp.dot(misfit, col_fac, precision=highest), 'col')  55.3 us
  transfers between devices with their start and end apart: 8, of which 8 were waited for; matrix products, arithmetic and copies ran while one was open for 0% of the time, Pallas kernels for 0%

profile of v1, /device:TPU:32, one launch (start us, length us, event | category | flops | bytes accessed | tf_op | source)
XLA Modules:
  0.0 2260.7 jit_solution(12492873241208168827)
XLA Ops:
  7.2 0.0 all-reduce.7.cloned.1.call-start
  7.2 1.0 convert_element_type.3
  8.2 0.1 copy.7
  8.3 1.5 broadcast_bitcast_fusion
  9.8 2.0 copy.10
  11.8 0.0 copy-done.8
  11.8 7.0 fusion
  18.7 65.8 %psum.119 = f32[]{:T(128)} all-reduce(f32[]{:T(128)} %get-tuple-element.12), channel_id=1, replica_groups=mesh['pix'=64,'col'=2] {'pix','col'}, use_global_device_ids=true, to_apply=%region_1.0 | all-reduce | flops 1 | bytes 8 | tf_op jit(solution)/shard_map/psum | solution.py:40
  85.2 5.7 fusion.20
  91.0 0.0 all-reduce.7.cloned.1.call-update
  91.0 0.0 all-reduce.9.cloned.1.call-start
  91.0 28.1 %all-reduce.7.cloned.1.call-done = f32[256,256]{1,0:T(8,128)} async-done(((f32[256,256]{1,0:T(8,128)}), f32[256,256]{1,0:T(8,128)}) %all-reduce.7.cloned.1.call-update) | async-done | bytes 262160 | tf_op jit(solution)/shard_map/psum | solution.py:79
  119.1 1.6 multiply_reduce_fusion.3
  120.7 5.6 fusion.1
  126.4 5.6 psum.122
  131.9 156.1 %all-reduce.1 = (f32[]{:T(128)}, f32[]{:T(128)}) all-reduce(f32[]{:T(128)} %multiply_reduce_fusion.3, f32[]{:T(128)} %psum.122), channel_id=1, replica_groups=mesh['pix'=64,'col'=2] {'pix'}, use_global_device_ids=true, to_apply=%region_4.0 | all-reduce | flops 2 | bytes 16 | tf_op jit(solution)/shard_map/psum | solution.py:83
  289.3 9.0 fusion.16
  298.3 0.0 all-reduce.9.cloned.1.call-update
  298.4 0.0 all-reduce.11.cloned.1.call-start
  298.4 645.4 %all-reduce.9.cloned.1.call-done = f32[2048,256]{1,0:T(8,128)} async-done(((f32[2048,256]{1,0:T(8,128)}), f32[2048,256]{1,0:T(8,128)}) %all-reduce.9.cloned.1.call-update) | async-done | bytes 2097168 | tf_op jit(solution)/shard_map/psum | solution.py:96
  943.9 2.7 multiply_reduce_fusion.1
  946.6 5.5 psum.125
  952.1 5.5 fusion.2
  957.6 68.9 %psum.126 = f32[]{:T(128)} all-reduce(f32[]{:T(128)} %get-tuple-element.25), channel_id=1, replica_groups=mesh['pix'=64,'col'=2] {'pix','col'}, use_global_device_ids=true, to_apply=%region_12.0 | all-reduce | flops 1 | bytes 8 | tf_op jit(solution)/shard_map/psum | solution.py:101
  1027.8 7.4 fusion.3
  1035.3 64.7 %psum.127 = f32[]{:T(128)} all-reduce(f32[]{:T(128)} %get-tuple-element.9), channel_id=1, replica_groups=mesh['pix'=64,'col'=2] {'pix','col'}, use_global_device_ids=true, to_apply=%region_14.0 | all-reduce | flops 1 | bytes 8 | tf_op jit(solution)/shard_map/psum | solution.py:40
  1100.7 0.0 copy-start.3
  1100.7 2.6 multiply_subtract_fusion.2
  1103.4 1.3 copy-done
  1104.7 0.0 copy-done.3
  1104.7 3.5 fusion.11
  1108.2 0.0 all-reduce.11.cloned.1.call-update
  1108.3 0.0 all-reduce.13.cloned.1.call-start
  1108.3 27.3 %all-reduce.11.cloned.1.call-done = f32[256,256]{1,0:T(8,128)} async-done(((f32[256,256]{1,0:T(8,128)}), f32[256,256]{1,0:T(8,128)}) %all-reduce.11.cloned.1.call-update) | async-done | bytes 262160 | tf_op jit(solution)/shard_map/psum | solution.py:79
  1135.6 1.6 multiply_reduce_fusion.2
  1137.2 5.6 fusion.4
  1142.8 5.6 psum.130
  1148.4 155.7 %all-reduce = (f32[]{:T(128)}, f32[]{:T(128)}) all-reduce(f32[]{:T(128)} %multiply_reduce_fusion.2, f32[]{:T(128)} %psum.130), channel_id=1, replica_groups=mesh['pix'=64,'col'=2] {'pix'}, use_global_device_ids=true, to_apply=%region_17.0 | all-reduce | flops 2 | bytes 16 | tf_op jit(solution)/shard_map/psum | solution.py:83
  1305.4 0.0 copy-done.5
  1305.5 0.0 copy-start.4
  1305.5 9.1 fusion.7
  1314.6 0.0 all-reduce.13.cloned.1.call-update
  1314.6 645.5 %all-reduce.13.cloned.1.call-done = f32[2048,256]{1,0:T(8,128)} async-done(((f32[2048,256]{1,0:T(8,128)}), f32[2048,256]{1,0:T(8,128)}) %all-reduce.13.cloned.1.call-update) | async-done | bytes 2097168 | tf_op jit(solution)/shard_map/psum | solution.py:96
  1960.1 2.7 multiply_reduce_fusion
  1962.9 5.8 psum.133
  1968.6 5.5 fusion.5
  1974.1 69.0 %psum.134 = f32[]{:T(128)} all-reduce(f32[]{:T(128)} %get-tuple-element.29), channel_id=1, replica_groups=mesh['pix'=64,'col'=2] {'pix','col'}, use_global_device_ids=true, to_apply=%region_25.0 | all-reduce | flops 1 | bytes 8 | tf_op jit(solution)/shard_map/psum | solution.py:101
  2044.4 6.5 fusion.6
  2050.9 64.4 %psum.135 = f32[]{:T(128)} all-reduce(f32[]{:T(128)} %get-tuple-element.7), channel_id=1, replica_groups=mesh['pix'=64,'col'=2] {'pix','col'}, use_global_device_ids=true, to_apply=%region_27.0 | all-reduce | flops 1 | bytes 8 | tf_op jit(solution)/shard_map/psum | solution.py:40
  2116.0 3.7 multiply_multiply_fusion.7
  2119.7 3.5 collective-permute-start.1
  2123.2 1.9 collective-permute-start
  2125.2 0.9 slice_bitcast_fusion.7
  2126.1 2.5 slice_bitcast_fusion.3
  2128.6 38.5 %collective-permute-done.1 = f32[256,2048]{1,0:T(8,128)S(1)} collective-permute-done((f32[256,2048]{1,0:T(8,128)}, f32[256,2048]{1,0:T(8,128)S(1)}, u32[]{:S(2)}, u32[]{:S(2)}) %collective-permute-start.1) | collective-permute-done | bytes 2097184 | tf_op jit(solution)/shard_map/ppermute | solution.py:28
  2167.1 4.2 collective-permute-done
  2171.4 4.4 multiply_add_fusion.1
  2175.8 3.2 collective-permute-start.3
  2179.0 1.9 collective-permute-start.2
  2180.9 1.6 multiply_subtract_fusion
  2182.5 0.4 slice_bitcast_fusion.1
  2183.0 39.8 %collective-permute-done.3 = f32[256,2048]{1,0:T(8,128)S(1)} collective-permute-done((f32[256,2048]{1,0:T(8,128)S(1)}, f32[256,2048]{1,0:T(8,128)S(1)}, u32[]{:S(2)}, u32[]{:S(2)}) %collective-permute-start.3) | collective-permute-done | bytes 2097184 | tf_op jit(solution)/shard_map/ppermute | solution.py:28
  2222.7 27.9 %collective-permute-done.2 = f32[256,2048]{1,0:T(8,128)S(1)} collective-permute-done((f32[256,2048]{1,0:T(8,128)S(1)}, f32[256,2048]{1,0:T(8,128)S(1)}, u32[]{:S(2)}, u32[]{:S(2)}) %collective-permute-start.2) | collective-permute-done | bytes 2097184 | tf_op jit(solution)/shard_map/ppermute | solution.py:28
  2250.6 3.3 multiply_add_fusion
  (15 shorter events, 0.1 us)
Async XLA Ops:
  7.2 111.9 %all-reduce.7.cloned.1.call-start = ((), (), s32[]{:S(2)}) async-start(), calls=%async_computation | async-start | bytes 524288 | tf_op jit(solution)/shard_map/psum | solution.py:79
  9.8 2.0 copy-start.8
  91.0 852.9 %all-reduce.9.cloned.1.call-start = ((), (), s32[]{:S(2)}) async-start(), calls=%async_computation.1 | async-start | bytes 4194304 | tf_op jit(solution)/shard_map/psum | solution.py:96
  120.7 168.5 %copy-start.6 = (f32[256,256]{1,0:T(8,128)S(1)}, f32[256,256]{1,0:T(8,128)}, u32[]{:S(2)}) copy-start(f32[256,256]{1,0:T(8,128)} %all-reduce.7.cloned.1.call-done) | copy-start | bytes 786436
  298.4 837.2 %all-reduce.11.cloned.1.call-start = ((), (), s32[]{:S(2)}) async-start(), calls=%async_computation.2 | async-start | bytes 524288 | tf_op jit(solution)/shard_map/psum | solution.py:79
  1100.7 4.0 copy-start.3
  1103.4 1.4 copy-start
  1108.3 851.9 %all-reduce.13.cloned.1.call-start = ((), (), s32[]{:S(2)}) async-start(), calls=%async_computation.3 | async-start | bytes 4194304 | tf_op jit(solution)/shard_map/psum | solution.py:96
  1137.2 168.2 %copy-start.5 = (f32[256,256]{1,0:T(8,128)S(1)}, f32[256,256]{1,0:T(8,128)}, u32[]{:S(2)}) copy-start(f32[256,256]{1,0:T(8,128)} %all-reduce.11.cloned.1.call-done) | copy-start | bytes 786436
  1305.5 663.1 %copy-start.4 = (f32[256,256]{1,0:T(8,128)}, f32[256,256]{1,0:T(8,128)S(1)}, u32[]{:S(2)}) copy-start(f32[256,256]{1,0:T(8,128)S(1)} %multiply_subtract_fusion.7) | copy-start | bytes 786436
  2119.7 47.5 %collective-permute-start.1 = (f32[256,2048]{1,0:T(8,128)}, f32[256,2048]{1,0:T(8,128)S(1)}, u32[]{:S(2)}, u32[]{:S(2)}) collective-permute-start(f32[256,2048]{1,0:T(8,128)} %multiply_multiply_fusion.7), channel_id=1, source_target_pairs={{2,0},{4,2},{6,4},{8,6},{10,8},{12,10},{14,12},{16,14},{18,16},{20... | collective-permute-start | bytes 6291464 | tf_op jit(solution)/shard_map/ppermute | solution.py:28
  2123.2 48.2 %collective-permute-start = (f32[256,2048]{1,0:T(8,128)}, f32[256,2048]{1,0:T(8,128)}, u32[]{:S(2)}, u32[]{:S(2)}) collective-permute-start(f32[256,2048]{1,0:T(8,128)} %multiply_multiply_fusion.7), channel_id=1, source_target_pairs={{0,2},{2,4},{4,6},{6,8},{8,10},{10,12},{12,14},{14,16},{16,18},{18... | collective-permute-start | bytes 6291464 | tf_op jit(solution)/shard_map/ppermute | solution.py:28
  2167.1 4.3 copy-start.7
  2171.4 9.5 copy-start.1
  2171.4 9.5 copy-start.2
  2175.8 47.0 %collective-permute-start.3 = (f32[256,2048]{1,0:T(8,128)S(1)}, f32[256,2048]{1,0:T(8,128)S(1)}, u32[]{:S(2)}, u32[]{:S(2)}) collective-permute-start(f32[256,2048]{1,0:T(8,128)S(1)} %multiply_add_fusion.1), channel_id=1, source_target_pairs={{2,0},{4,2},{6,4},{8,6},{10,8},{12,10},{14,12},{16,14},{18,16},{20... | collective-permute-start | bytes 6291464 | tf_op jit(solution)/shard_map/ppermute | solution.py:28
  2179.0 71.6 %collective-permute-start.2 = (f32[256,2048]{1,0:T(8,128)S(1)}, f32[256,2048]{1,0:T(8,128)S(1)}, u32[]{:S(2)}, u32[]{:S(2)}) collective-permute-start(f32[256,2048]{1,0:T(8,128)S(1)} %multiply_add_fusion.1), channel_id=1, source_target_pairs={{0,2},{2,4},{4,6},{6,8},{8,10},{10,12},{12,14},{14,16},{16,18},{18... | collective-permute-start | bytes 6291464 | tf_op jit(solution)/shard_map/ppermute | solution.py:28
Sparse Core Ops, SparseCore 0:
  91.1 27.9 all-reduce.6
  298.5 645.3 all-reduce.8
  1108.4 27.1 all-reduce.10
  1314.7 645.3 all-reduce.12
